TPU v7x, 256 devices: a whole 4x4x8 slice. The times are simulated.
256 devices in a mesh: wide: 64 (over z, x, core), narrow: 4 (over y).
Axes of the slice: x: 4, y: 4, z: 8, core: 2. Of those that a mesh axis runs over, the one named last changes fastest.
Arguments:
- coeffs: bfloat16 [2, 1024, 1024, 512], P(None, 'wide', None, 'narrow'), may hold values from -3 to 3
- legendre: bfloat16 [1024, 64, 1024], P('wide'), may hold values from -3 to 3
- order_table: int32 [1024], replicated, may hold values from 0 to 1023, each once
- thresholds: float32 [512], replicated, may hold values from 0.2 to 2
Outputs:
- lowrank: float32 [64, 2048, 512], P('wide', 'narrow')
- sparse: float32 [64, 2048, 512], P('wide', 'narrow')
Inputs may be any that keep to these rules, and one draw needn't show every extreme that they name: `order_table`: each order 0 to 1023 stands in exactly one slot.
All inputs are finite; a program needn't handle non-finite values.
Results may differ from a plain program's by a relative error of at most 0.0003.
Values sent between devices are 32-bit elements; how exact they have to be, the bound alone decides.
A program may use at most 128 MiB of HBM per device.

v0:
```python
import math

import jax
import jax.numpy as jnp
from jax import lax
from jax.sharding import PartitionSpec as P

NPIX = 2048
ITERS = 2


def soft_shrink(values, limits):
    return jnp.sign(values) * jnp.maximum(jnp.abs(values) - limits, 0.0)


def wiener_filter(covariance):
    chan_total = covariance.shape[0]
    ridge_shift = jnp.trace(covariance) / chan_total
    factor = jnp.linalg.cholesky(
        covariance + ridge_shift * jnp.eye(chan_total, dtype=covariance.dtype)
    )
    return jax.scipy.linalg.cho_solve((factor, True), covariance)


def per_device(coeffs, legendre, order_table, thresholds):
    slot_count = legendre.shape[0]
    degrees = legendre.shape[2]
    first_slot = lax.axis_index("wide") * slot_count
    own_orders = lax.dynamic_slice_in_dim(order_table, first_slot, slot_count)
    degree_mask = (
        lax.broadcasted_iota(jnp.int32, (slot_count, degrees), 1) >= own_orders[:, None]
    ).astype(legendre.dtype)
    masked = legendre * degree_mask[:, None, :]
    spectra = jnp.einsum("srl,kslc->ksrc", masked, coeffs, preferred_element_type=jnp.float32)
    pixels = lax.broadcasted_iota(jnp.int32, (1, NPIX), 1)
    pixel_phase = order_table[:, None] * pixels % NPIX
    pixel_angle = pixel_phase.astype(jnp.float32) * (2.0 * math.pi / NPIX)
    weights = jnp.where(order_table == 0, 1.0, 2.0).astype(jnp.float32)[:, None]
    cycle_table = jnp.stack([weights * jnp.cos(pixel_angle), -weights * jnp.sin(pixel_angle)])
    sky_map = jnp.einsum(
        "ksrc,ksj->rjc",
        lax.all_to_all(spectra, "wide", split_axis=2, concat_axis=1, tiled=True),
        cycle_table,
        precision=lax.Precision.HIGHEST,
        preferred_element_type=jnp.float32,
    )
    spectra_rows = lax.all_to_all(sky_map, "narrow", split_axis=1, concat_axis=2, tiled=True)
    cycle_count, pixel_count, chan_count = spectra_rows.shape
    sky_field = spectra_rows.reshape(cycle_count * pixel_count, chan_count)
    lowrank = jnp.zeros_like(sky_field)
    sparse = jnp.zeros_like(sky_field)
    for iteration in range(ITERS):
        sparse = soft_shrink(sky_field - lowrank, thresholds)
        residue = sky_field - sparse
        partial_cov = jnp.dot(
            residue.T, residue, precision=lax.Precision.HIGHEST, preferred_element_type=jnp.float32
        )
        covariance = lax.psum(partial_cov, ("wide", "narrow"))
        lowrank = jnp.dot(
            residue,
            wiener_filter(covariance),
            precision=lax.Precision.HIGHEST,
            preferred_element_type=jnp.float32,
        )
    return (
        lowrank.reshape(cycle_count, pixel_count, chan_count),
        sparse.reshape(cycle_count, pixel_count, chan_count),
    )


def solution(mesh):
    placed = (P(None, "wide", None, "narrow"), P("wide", None, None), P(), P())
    return jax.shard_map(
        per_device,
        mesh=mesh,
        in_specs=placed,
        out_specs=(P("wide", "narrow", None), P("wide", "narrow", None)),
        check_vma=False,
    )
```

profile of v0, /device:TPU:1, one launch (start us, length us, event | category | flops | bytes accessed | tf_op | source)
XLA Modules:
  0.0 965.8 jit_solution(3870654779187750146)
XLA Ops:
  15.3 13.0 %all-to-all-start = ((f32[2,16,64,128]{3,0,1,2:T(2,128)}), f32[2,16,64,128]{3,0,1,2:T(2,128)S(1)}, u32[]{:S(2)}, u32[]{:S(2)}) async-start(f32[2,16,64,128]{3,0,1,2:T(2,128)} %copy.24), calls=%async_computation | async-start | bytes 2097152 | tf_op jit(solution)/shard_map/all_to_all | solution.py:42
  28.3 35.0 %cosine_multiply_fusion = (f32[1,1024,2048]{1,2,0:T(8,128)}, f32[1,1024,2048]{1,2,0:T(8,128)}) fusion(s32[1024]{0:T(1024)S(1)} %copy-done.7, f32[1024]{0:T(1024)S(1)} %get-tuple-element.68, f32[1024]{0:T(1024)S(1)} %get-tuple-element.69), kind=kLoop, calls=%fused_computation.17 | loop fusion | flops 33554432 | bytes 16789504 | tf_op jit(solution)/shard_map/mul | solution.py:39
  63.4 16.5 %fusion = f32[2048,128,1]{1,0,2:T(8,128)S(1)} fusion(f32[2,1024,128]{2,1,0:T(8,128)S(1)} %bitcast.179, f32[1,1024,2048]{1,2,0:T(8,128)} %get-tuple-element.67, f32[1,1024,2048]{1,2,0:T(8,128)} %get-tuple-element.66), kind=kOutput, calls=%fused_computation.4 | convolution fusion | flops 6446645248 | bytes 18874368 | tf_op jit(solution)/shard_map/ksrc,ksj->rjc/dot_general | solution.py:40
  80.0 18.4 %all_to_all.30 = f32[1,2048,128]{2,0,1:T(1,128)S(1)} all-to-all(f32[1,2048,128]{2,0,1:T(1,128)S(1)} %bitcast.180), channel_id=1, replica_groups=mesh['wide'=64,'narrow'=4] {'narrow'}, dimensions={1} | all-to-all | bytes 2097152 | tf_op jit(solution)/shard_map/all_to_all | solution.py:47
  103.4 256.6 %all-reduce.4.cloned.1.call-done = f32[512,512]{0,1:T(8,128)} async-done(((f32[512,512]{0,1:T(8,128)}), f32[512,512]{0,1:T(8,128)}) %all-reduce.4.cloned.1.call-update) | async-done | bytes 1048592 | tf_op jit(solution)/shard_map/psum | solution.py:58
  368.1 11.7 %cholesky.286 = f32[128,128]{1,0:T(8,128)S(1)} custom-call(f32[128,128]{1,0:T(8,128)S(1)} %cholesky.426), custom_call_target="Cholesky" | custom-call | tf_op jit(solution)/shard_map/jit(cholesky)/cholesky | solution.py:19
  379.8 9.8 %custom-call.29 = f32[1,128,128]{1,2,0:T(8,128)S(1)} custom-call(f32[1,128,128]{2,1,0:T(8,128)S(1)} %get-tuple-element.65), custom_call_target="InvertDiagBlocksLowerTriangular" | custom-call | tf_op jit(solution)/shard_map/jit(cholesky)/cholesky | solution.py:19
  392.3 11.7 %cholesky.305 = f32[128,128]{1,0:T(8,128)S(1)} custom-call(f32[128,128]{1,0:T(8,128)S(1)} %cholesky.430), custom_call_target="Cholesky" | custom-call | tf_op jit(solution)/shard_map/jit(cholesky)/cholesky | solution.py:19
  404.0 18.5 %custom-call.30 = f32[1,128,128]{1,2,0:T(8,128)S(1)} custom-call(f32[1,128,128]{2,1,0:T(8,128)S(1)} %get-tuple-element.62), custom_call_target="InvertDiagBlocksLowerTriangular" | custom-call | tf_op jit(solution)/shard_map/jit(cholesky)/cholesky | solution.py:19
  424.1 11.7 %cholesky.326 = f32[128,128]{1,0:T(8,128)S(1)} custom-call(f32[128,128]{1,0:T(8,128)S(1)} %cholesky.435), custom_call_target="Cholesky" | custom-call | tf_op jit(solution)/shard_map/jit(cholesky)/cholesky | solution.py:19
  436.5 9.8 %custom-call.31 = f32[1,128,128]{1,2,0:T(8,128)S(1)} custom-call(f32[1,128,128]{2,1,0:T(8,128)S(1)} %get-tuple-element.59), custom_call_target="InvertDiagBlocksLowerTriangular" | custom-call | tf_op jit(solution)/shard_map/jit(cholesky)/cholesky | solution.py:19
  447.8 12.1 %cholesky.343 = f32[128,128]{1,0:T(8,128)S(1)} custom-call(f32[128,128]{1,0:T(8,128)S(1)} %convolution_subtract_fusion.18), custom_call_target="Cholesky" | custom-call | tf_op jit(solution)/shard_map/jit(cholesky)/cholesky | solution.py:19
  464.9 11.2 %while.4 = (s32[]{:T(128)}, f32[512,512]{1,0:T(8,128)}, s32[4,2]{0,1:T(2,128)S(1)}, f32[4,128,128]{2,1,0:T(8,128)S(1)}, s32[]{:T(128)}) while((s32[]{:T(128)}, f32[512,512]{1,0:T(8,128)}, s32[4,2]{0,1:T(2,128)S(1)}, f32[4,128,128]{2,1,0:T(8,128)S(1)}, s32[]{:T(128)}) %tuple.61), condition=%wide.while_cond, body=%wide.while_body.sunk | while | flops 2 | bytes 131181 | solution.py:22
  476.9 40.1 %custom-call.32 = f32[4,128,128]{1,2,0:T(8,128)S(1)} custom-call(f32[4,128,128]{2,1,0:T(8,128)} %copy-done.5), custom_call_target="InvertDiagBlocksLowerTriangular" | custom-call | tf_op jit(solution)/shard_map/jit(_cho_solve)/triangular_solve | solution.py:22
  538.9 255.4 %all-reduce.6.cloned.1.call-done = f32[512,512]{0,1:T(8,128)} async-done(((f32[512,512]{0,1:T(8,128)}), f32[512,512]{0,1:T(8,128)}) %all-reduce.6.cloned.1.call-update) | async-done | bytes 1048592 | tf_op jit(solution)/shard_map/psum | solution.py:58
  802.4 11.9 %cholesky.358 = f32[128,128]{1,0:T(8,128)S(1)} custom-call(f32[128,128]{1,0:T(8,128)S(1)} %cholesky.439), custom_call_target="Cholesky" | custom-call | tf_op jit(solution)/shard_map/jit(cholesky)/cholesky | solution.py:19
  814.4 9.8 %custom-call.33 = f32[1,128,128]{1,2,0:T(8,128)S(1)} custom-call(f32[1,128,128]{2,1,0:T(8,128)S(1)} %get-tuple-element.55), custom_call_target="InvertDiagBlocksLowerTriangular" | custom-call | tf_op jit(solution)/shard_map/jit(cholesky)/cholesky | solution.py:19
  826.8 11.7 %cholesky.377 = f32[128,128]{1,0:T(8,128)S(1)} custom-call(f32[128,128]{1,0:T(8,128)S(1)} %cholesky.443), custom_call_target="Cholesky" | custom-call | tf_op jit(solution)/shard_map/jit(cholesky)/cholesky | solution.py:19
  839.9 10.0 %custom-call.34 = f32[1,128,128]{1,2,0:T(8,128)S(1)} custom-call(f32[1,128,128]{2,1,0:T(8,128)S(1)} %get-tuple-element.52), custom_call_target="InvertDiagBlocksLowerTriangular" | custom-call | tf_op jit(solution)/shard_map/jit(cholesky)/cholesky | solution.py:19
  851.4 11.7 %cholesky.398 = f32[128,128]{1,0:T(8,128)S(1)} custom-call(f32[128,128]{1,0:T(8,128)S(1)} %cholesky.448), custom_call_target="Cholesky" | custom-call | tf_op jit(solution)/shard_map/jit(cholesky)/cholesky | solution.py:19
  863.9 9.8 %custom-call.35 = f32[1,128,128]{1,2,0:T(8,128)S(1)} custom-call(f32[1,128,128]{2,1,0:T(8,128)S(1)} %get-tuple-element.49), custom_call_target="InvertDiagBlocksLowerTriangular" | custom-call | tf_op jit(solution)/shard_map/jit(cholesky)/cholesky | solution.py:19
  875.1 11.7 %cholesky.415 = f32[128,128]{1,0:T(8,128)S(1)} custom-call(f32[128,128]{1,0:T(8,128)S(1)} %convolution_subtract_fusion.17), custom_call_target="Cholesky" | custom-call | tf_op jit(solution)/shard_map/jit(cholesky)/cholesky | solution.py:19
  891.2 11.7 %while.5 = (s32[]{:T(128)}, f32[512,512]{1,0:T(8,128)}, s32[4,2]{0,1:T(2,128)S(1)}, f32[4,128,128]{2,1,0:T(8,128)S(1)}, s32[]{:T(128)}) while((s32[]{:T(128)}, f32[512,512]{1,0:T(8,128)}, s32[4,2]{0,1:T(2,128)S(1)}, f32[4,128,128]{2,1,0:T(8,128)S(1)}, s32[]{:T(128)}) %tuple.71), condition=%wide.while_cond.clone, body=%wide.while_body.clone.sunk | while | flops 2 | bytes 131181 | solution.py:22
  902.9 39.6 %custom-call.36 = f32[4,128,128]{1,2,0:T(8,128)S(1)} custom-call(f32[4,128,128]{2,1,0:T(8,128)S(1)} %get-tuple-element.19), custom_call_target="InvertDiagBlocksLowerTriangular" | custom-call | tf_op jit(solution)/shard_map/jit(_cho_solve)/triangular_solve | solution.py:22
  (136 shorter events, 107.6 us)
Async XLA Ops:
  8.0 20.3 %copy-start.7 = (s32[1024]{0:T(1024)S(1)}, s32[1024]{0:T(1024)}, u32[]{:S(2)}) copy-start(s32[1024]{0:T(1024)} %param.9) | copy-start | bytes 12292
  15.3 48.0 %all-to-all-start = ((f32[2,16,64,128]{3,0,1,2:T(2,128)}), f32[2,16,64,128]{3,0,1,2:T(2,128)S(1)}, u32[]{:S(2)}, u32[]{:S(2)}) async-start(f32[2,16,64,128]{3,0,1,2:T(2,128)} %copy.24), calls=%async_computation | async-start | bytes 2097152 | tf_op jit(solution)/shard_map/all_to_all | solution.py:42
  28.2 331.8 %all-reduce.4.cloned.1.call-start = ((), (), s32[]{:S(2)}) async-start(), calls=%async_computation.2 | async-start | bytes 2097152 | tf_op jit(solution)/shard_map/psum | solution.py:58
  63.4 35.3 %copy-start.6 = (f32[512]{0:T(512)S(1)}, f32[512]{0:T(512)}, u32[]{:S(2)}) copy-start(f32[512]{0:T(512)} %param.10) | copy-start | bytes 6148
  102.0 692.4 %all-reduce.6.cloned.1.call-start = ((), (), s32[]{:S(2)}) async-start(), calls=%async_computation.3 | async-start | bytes 2097152 | tf_op jit(solution)/shard_map/psum | solution.py:58
  360.0 157.0 %copy-start = (f32[512,512]{0,1:T(8,128)S(1)}, f32[512,512]{0,1:T(8,128)}, u32[]{:S(2)}) copy-start(f32[512,512]{0,1:T(8,128)} %all-reduce.4.cloned.1.call-done) | copy-start | bytes 3145732
  367.1 1.0 copy-start.4
  464.9 65.3 %copy-start.2 = (f32[512,512]{0,1:T(8,128)S(1)}, f32[512,512]{0,1:T(8,128)}, u32[]{:S(2)}) copy-start(f32[512,512]{0,1:T(8,128)} %bitcast_subtract_fusion.1) | copy-start | bytes 3145732
  476.1 0.7 copy-start.5
  794.4 148.1 %copy-start.1 = (f32[512,512]{0,1:T(8,128)S(1)}, f32[512,512]{0,1:T(8,128)}, u32[]{:S(2)}) copy-start(f32[512,512]{0,1:T(8,128)} %all-reduce.6.cloned.1.call-done) | copy-start | bytes 3145732
  801.4 1.0 copy-start.3
Sparse Core Ops, SparseCore 0:
  102.1 257.8 all-reduce.3
  536.5 257.8 all-reduce.5
where the time goes:
time: 975 us; the launch traced here: 966 us
  waiting for transfers between devices  512 us (53%)
  other arithmetic  296 us (30%)
  matrix products  71 us (7%)
  local copies, waits for them, and re-layouts  33.9 us (3%)
  between operations  21.4 us (2%)
  blocking collectives  18.4 us (2%)
  starting transfers between devices  13.1 us (1%)
    psum x2, waiting for transfers between devices, per_device(): covariance = lax.psum(partial_cov, ('wide', 'narrow'))  512 us
    another operation x29, other arithmetic, wiener_filter(): jnp.linalg.cholesky(covariance + ridge_shift * jnp.eye(chan_total, dtype=...  167 us
    another operation x5, other arithmetic, wiener_filter(): return jax.scipy.linalg.cho_solve((factor, True), covariance)  81.9 us
    mul x1, other arithmetic, per_device(): weights * jnp.cos(pixel_angle)  35 us
    another operation x28, matrix products, wiener_filter(): return jax.scipy.linalg.cho_solve((factor, True), covariance)  26.2 us
    another operation x27, local copies, waits for them, and re-layouts, wiener_filter(): return jax.scipy.linalg.cho_solve((factor, True), covariance)  22.8 us
  transfers between devices with their start and end apart: 3, of which 2 were waited for; matrix products, arithmetic and copies ran while one was open for 4% of the time, Pallas kernels for 0%

commit v1 on v0

v1 whole, which is shorter than its diff:
```python
import functools
import math

import jax
import jax.numpy as jnp
from jax import lax
from jax.experimental import pallas as pl
from jax.experimental.pallas import tpu as pltpu
from jax.sharding import PartitionSpec as P

MESH = pl.DeviceIdType.MESH
F32 = jnp.float32
BF16 = jnp.bfloat16

NPIX = 2048
NCH = 512
NB = 4
PAIRS = [(i, j) for i in range(NB) for j in range(i, NB)]
ROWS = 128 * len(PAIRS)
HALF = ROWS // 2
X, Y, Z = 4, 4, 8
CHUNK = HALF // (X * Y)
LIMIT = 64 * 1024 * 1024 - 65536 - 8192

KAPPA = NCH + 1.0
OMEGA = 2.0 / (KAPPA + 1.0)


def newton_scales():
    delta = (KAPPA - 1.0) / (KAPPA + 1.0)
    scales = []
    while delta > 1e-4:
        scales.append(2.0 / (2.0 - delta * delta))
        delta = delta * delta / (2.0 - delta * delta)
    return scales


SCALES = newton_scales()


def split(x):
    hi = x.astype(BF16)
    return hi, (x - hi.astype(F32)).astype(BF16)


def dot(a, b):
    return jnp.dot(a, b, preferred_element_type=F32)


def put_left(ref, x):
    n = x.shape[1]
    hi, lo = split(x)
    ref[:, 0:n] = hi
    ref[:, n : 2 * n] = lo
    ref[:, 2 * n : 3 * n] = hi


def put_right(ref, x):
    n = x.shape[0]
    hi, lo = split(x)
    ref[0:n, :] = hi
    ref[n : 2 * n, :] = hi
    ref[2 * n : 3 * n, :] = lo


def reduce_kernel(p_ref, out_ref, b1, acc1, b2, acc2, b3, acc3, s1, r1, s2, r2, s3, r3, s4, r4, s5, r5):
    w = lax.axis_index("wide")
    y = lax.axis_index("narrow")
    core = lax.rem(w, 2)
    x = lax.rem(w // 2, X)
    z = w // (2 * X)
    other = 1 - core
    partner = (w + 1 - 2 * core, y)

    def plane(k):
        dx, dy = k // Y, k % Y
        px, py = lax.rem(x + dx, X), lax.rem(y + dy, Y)
        return (z * 2 * X + px * 2 + core, py), px * Y + py

    def deep(d):
        return (lax.rem(z + d, Z) * 2 * X + x * 2 + core, y)

    barrier = pltpu.get_barrier_semaphore()
    peers = [partner] + [plane(k)[0] for k in range(1, X * Y)] + [deep(d) for d in range(1, Z)]
    for peer in peers:
        pl.semaphore_signal(barrier, inc=1, device_id=peer, device_id_type=MESH)
    pl.semaphore_wait(barrier, len(peers))

    order = sorted(range(X * Y), key=lambda k: -(min(k // Y, X - k // Y) + min(k % Y, Y - k % Y)))

    def rows(side, g):
        return pl.ds(pl.multiple_of(side * HALF + g * CHUNK, 8), CHUNK)

    def remote(src, dst, send, recv, peer):
        return pltpu.make_async_remote_copy(
            src_ref=src, dst_ref=dst, send_sem=send, recv_sem=recv, device_id=peer, device_id_type=MESH
        )

    first, second = {}, {}
    for k in order:
        first[k] = remote(p_ref.at[rows(other, plane(k)[1])], b1.at[k], s1.at[k], r1.at[k], partner)
        first[k].start()
    for k in order:
        peer, g = plane(k)
        first[k].wait_recv()
        acc1[k] = p_ref[rows(core, g)] + b1[k]
        if k:
            second[k] = remote(acc1.at[k], b2.at[k], s2.at[k], r2.at[k], peer)
            second[k].start()
    total = acc1[0]
    for k in order:
        if k:
            second[k].wait_recv()
            total = total + b2[k]
    acc2[...] = total
    third = {}
    for d in (4, 3, 5, 2, 6, 1, 7):
        third[d] = remote(acc2, b3.at[d], s3.at[d], r3.at[d], deep(d))
        third[d].start()
    total = acc2[...]
    for d in (1, 7, 2, 6, 3, 5, 4):
        third[d].wait_recv()
        total = total + b3[d]
    acc3[...] = total
    mine = rows(core, x * Y + y)
    fourth, fifth = {}, {}
    for k in order:
        if k:
            fourth[k] = remote(acc3, out_ref.at[mine], s4.at[k], r4.at[k], plane(k)[0])
            fourth[k].start()
    fifth[0] = remote(acc3, out_ref.at[mine], s5.at[0], r5.at[0], partner)
    fifth[0].start()
    out_ref[mine] = total
    for k in reversed(order):
        if k:
            px, py = lax.rem(x + X - k // Y, X), lax.rem(y + Y - k % Y, Y)
            got = rows(core, px * Y + py)
            fourth[k].wait_recv()
            fifth[k] = remote(out_ref.at[got], out_ref.at[got], s5.at[k], r5.at[k], partner)
            fifth[k].start()
    for k in order:
        fifth[k].wait_recv()
    for k in order:
        first[k].wait_send()
        fifth[k].wait_send()
        if k:
            second[k].wait_send()
            fourth[k].wait_send()
    for d in range(1, Z):
        third[d].wait_send()


def reduce_packed(packed):
    n = X * Y
    dma = pltpu.SemaphoreType.DMA
    return pl.pallas_call(
        reduce_kernel,
        name="reduce_packed",
        out_shape=jax.ShapeDtypeStruct((ROWS, 128), F32),
        in_specs=[pl.BlockSpec(memory_space=pltpu.VMEM)],
        out_specs=pl.BlockSpec(memory_space=pltpu.VMEM),
        scratch_shapes=[
            pltpu.VMEM((n, CHUNK, 128), F32),
            pltpu.VMEM((n, CHUNK, 128), F32),
            pltpu.VMEM((n, CHUNK, 128), F32),
            pltpu.VMEM((CHUNK, 128), F32),
            pltpu.VMEM((Z, CHUNK, 128), F32),
            pltpu.VMEM((CHUNK, 128), F32),
        ]
        + [dma((n,))] * 4
        + [dma((Z,))] * 2
        + [dma((n,))] * 4,
        compiler_params=pltpu.CompilerParams(collective_id=0, has_side_effects=True),
    )(packed)


def put_cov(res, cov_ref, left, right):
    put_right(left, res)
    n = res.shape[0]
    right[0:n, :] = left[0:n, :]
    right[n : 2 * n, :] = left[2 * n : 3 * n, :]
    right[2 * n : 3 * n, :] = left[0:n, :]
    at = 0
    for i in range(NB):
        width = (NB - i) * 128
        rows = lax.dot_general(
            left[:, i * 128 : (i + 1) * 128],
            right[:, i * 128 :],
            (((0,), (0,)), ((), ())),
            preferred_element_type=F32,
        )
        for b in range(NB - i):
            cov_ref[at : at + 128, :] = rows[:, b * 128 : (b + 1) * 128]
            at += 128


def first_kernel(sky_ref, thr_ref, res_ref, cov_ref, left, right):
    thr = thr_ref[...]
    sky = sky_ref[...]
    res = sky - (sky - jnp.minimum(jnp.maximum(sky, -thr), thr))
    res_ref[...] = res
    put_cov(res, cov_ref, left, right)


def put_inverse(cov_ref, scales_ref, a_ref, x_ref, a3, xl, xr):
    eye = (lax.broadcasted_iota(jnp.int32, (128, 128), 0) == lax.broadcasted_iota(jnp.int32, (128, 128), 1)).astype(F32)
    diag = jnp.zeros((128, 128), F32)
    for idx, (i, j) in enumerate(PAIRS):
        if i == j:
            diag = diag + cov_ref[idx * 128 : (idx + 1) * 128, :] * eye
    total = jnp.sum(jnp.sum(diag, axis=0, keepdims=True), axis=1, keepdims=True)
    inv_t = float(NCH) / total
    for idx, (i, j) in enumerate(PAIRS):
        block = cov_ref[idx * 128 : (idx + 1) * 128, :] * inv_t
        if i == j:
            block = block + eye
            a_ref[i * 128 : (i + 1) * 128, i * 128 : (i + 1) * 128] = block
        else:
            a_ref[i * 128 : (i + 1) * 128, j * 128 : (j + 1) * 128] = block
            a_ref[j * 128 : (j + 1) * 128, i * 128 : (i + 1) * 128] = block.T
    a = a_ref[...]
    put_right(a3, a)
    full_eye = (
        lax.broadcasted_iota(jnp.int32, (NCH, NCH), 0) == lax.broadcasted_iota(jnp.int32, (NCH, NCH), 1)
    ).astype(F32)
    x = (SCALES[0] * OMEGA) * (2.0 * full_eye - OMEGA * a)
    x_ref[...] = x
    put_left(xl, x)
    put_right(xr, x)

    def step(k, carry):
        wa = dot(xl[...], a3[...])
        put_left(xl, wa)
        x = scales_ref[k] * (2.0 * x_ref[...] - dot(xl[...], xr[...]))
        x_ref[...] = x
        put_left(xl, x)
        put_right(xr, x)
        return carry

    lax.fori_loop(1, len(SCALES), step, 0)
    x = x_ref[...]
    rest = full_eye - jnp.dot(x, a_ref[...], preferred_element_type=F32, precision=lax.Precision.HIGHEST)
    x = x + dot(rest.astype(BF16), xr[0:NCH, :])
    x_ref[...] = x
    put_right(xr, x)


def low_of(res_ref, xl, xr):
    res = res_ref[...]
    put_left(xl, res)
    return res - dot(xl[...], xr[...])


def middle_kernel(scales_ref, cov_ref, res_ref, sky_ref, thr_ref, sparse_ref, res2_ref, cov2_ref, a_ref, x_ref, a3, xl, xr):
    put_inverse(cov_ref, scales_ref, a_ref, x_ref, a3, xl, xr)
    thr = thr_ref[...]
    sky = sky_ref[...]
    v = sky - low_of(res_ref, xl, xr)
    sparse = v - jnp.minimum(jnp.maximum(v, -thr), thr)
    sparse_ref[...] = sparse
    res = sky - sparse
    res2_ref[...] = res
    put_cov(res, cov2_ref, a3, xr)


def last_kernel(scales_ref, cov_ref, res_ref, low_ref, a_ref, x_ref, a3, xl, xr):
    put_inverse(cov_ref, scales_ref, a_ref, x_ref, a3, xl, xr)
    low_ref[...] = low_of(res_ref, xl, xr)


VM = pl.BlockSpec(memory_space=pltpu.VMEM)
SM = pl.BlockSpec(memory_space=pltpu.SMEM)


def inverse_scratch():
    return [
        pltpu.VMEM((NCH, NCH), F32),
        pltpu.VMEM((NCH, NCH), F32),
        pltpu.VMEM((3 * NCH, NCH), BF16),
        pltpu.VMEM((NCH, 3 * NCH), BF16),
        pltpu.VMEM((3 * NCH, NCH), BF16),
    ]


def first_stage(sky, thr):
    pix = sky.shape[0]
    return pl.pallas_call(
        first_kernel,
        name="first_stage",
        out_shape=(jax.ShapeDtypeStruct((pix, NCH), F32), jax.ShapeDtypeStruct((ROWS, 128), F32)),
        in_specs=[VM, VM],
        out_specs=(VM, VM),
        scratch_shapes=[pltpu.VMEM((3 * pix, NCH), BF16), pltpu.VMEM((3 * pix, NCH), BF16)],
    )(sky, thr)


def middle_stage(scales, cov, res, sky, thr):
    pix = sky.shape[0]
    return pl.pallas_call(
        middle_kernel,
        name="middle_stage",
        out_shape=(
            jax.ShapeDtypeStruct((pix, NCH), F32),
            jax.ShapeDtypeStruct((pix, NCH), F32),
            jax.ShapeDtypeStruct((ROWS, 128), F32),
        ),
        in_specs=[SM, VM, VM, VM, VM],
        out_specs=(VM, VM, VM),
        scratch_shapes=inverse_scratch(),
    )(scales, cov, res, sky, thr)


def last_stage(scales, cov, res):
    return pl.pallas_call(
        last_kernel,
        name="last_stage",
        out_shape=jax.ShapeDtypeStruct(res.shape, F32),
        in_specs=[SM, VM, VM],
        out_specs=VM,
        scratch_shapes=inverse_scratch(),
    )(scales, cov, res)


SB = 64
HP = NPIX // 2
STEP = 4


def pixel_kernel(spec_ref, par_ref, coarse_ref, fine_ref, sky_ref, rhs):
    ns = spec_ref.shape[1]
    even = par_ref[...]
    for k in range(2):
        value = spec_ref[k]
        for p, part in enumerate((value * even, value * (1.0 - even))):
            hi, lo = split(part)
            rhs[k * ns : (k + 1) * ns, p * 128 : (p + 1) * 128] = hi
            rhs[k * ns : (k + 1) * ns, 256 + p * 128 : 256 + (p + 1) * 128] = lo

    def step(i, carry):
        tops = []
        for q in range(STEP):
            a = i * STEP + q
            ca = coarse_ref[0, pl.ds(a, 1), :]
            sa = coarse_ref[1, pl.ds(a, 1), :]
            cb, sb = fine_ref[0], fine_ref[1]
            tops.append(jnp.concatenate([ca * cb - sa * sb, -(sa * cb + ca * sb)], axis=1))
        table = jnp.concatenate(tops, axis=0)
        hi, lo = split(table)
        top = dot(hi, rhs[...])
        low = dot(lo, rhs[:, 0:256])
        e = top[:, 0:128] + top[:, 256:384] + low[:, 0:128]
        o = top[:, 128:256] + top[:, 384:512] + low[:, 128:256]
        j = pl.multiple_of(i * (STEP * SB), STEP * SB)
        sky_ref[pl.ds(j, STEP * SB), :] = e + o
        sky_ref[pl.ds(j + HP, STEP * SB), :] = e - o
        return carry

    lax.fori_loop(0, HP // (SB * STEP), step, 0)


def pixel_stage(spec, parity, coarse, fine):
    ns = spec.shape[1]
    return pl.pallas_call(
        pixel_kernel,
        name="pixel_stage",
        out_shape=jax.ShapeDtypeStruct((NPIX, spec.shape[2]), F32),
        in_specs=[VM, VM, VM, VM],
        out_specs=VM,
        scratch_shapes=[pltpu.VMEM((2 * ns, 512), BF16)],
    )(spec, parity, coarse, fine)


def per_device(coeffs, legendre, order_table, thresholds):
    slot_count = legendre.shape[0]
    degrees = legendre.shape[2]
    first_slot = lax.axis_index("wide") * slot_count
    own_orders = lax.dynamic_slice_in_dim(order_table, first_slot, slot_count)
    degree_mask = (
        lax.broadcasted_iota(jnp.int32, (slot_count, degrees), 1) >= own_orders[:, None]
    ).astype(legendre.dtype)
    masked = legendre * degree_mask[:, None, :]
    spectra = jnp.einsum("srl,kslc->ksrc", masked, coeffs, preferred_element_type=F32)
    spec = lax.all_to_all(spectra, "wide", split_axis=2, concat_axis=1, tiled=True)[:, :, 0, :]

    weights = jnp.where(order_table == 0, 1.0, 2.0).astype(F32)[None, :]

    def small_table(steps, stride, weight):
        at = lax.broadcasted_iota(jnp.int32, (steps, 1), 0) * stride
        angle = (order_table[None, :] * at % NPIX).astype(F32) * (2.0 * math.pi / NPIX)
        return jnp.stack([weight * jnp.cos(angle), weight * jnp.sin(angle)])

    coarse = small_table(HP // SB, SB, weights)
    fine = small_table(SB, 1, 1.0)
    parity = jnp.broadcast_to((1 - order_table % 2).astype(F32)[:, None], (order_table.shape[0], 128))
    sky_map = pixel_stage(spec, parity, coarse, fine)
    sky = lax.all_to_all(sky_map, "narrow", split_axis=0, concat_axis=1, tiled=True)
    thr = thresholds[None, :]
    scales = jnp.asarray(SCALES + [0.0] * (16 - len(SCALES)), F32)
    res, cov = first_stage(sky, thr)
    sparse, res, cov = middle_stage(scales, reduce_packed(cov), res, sky, thr)
    low = last_stage(scales, reduce_packed(cov), res)
    return low[None], sparse[None]


def solution(mesh):
    placed = (P(None, "wide", None, "narrow"), P("wide", None, None), P(), P())
    return jax.shard_map(
        per_device,
        mesh=mesh,
        in_specs=placed,
        out_specs=(P("wide", "narrow", None), P("wide", "narrow", None)),
        check_vma=False,
    )
```

time: 975 us -> 175 us (0.18)
  waiting for transfers between devices: 512 us -> 25.2 us
  other arithmetic: 296 us -> 2.97 us
  Pallas kernels: 0 us -> 104 us
  matrix products: 71 us -> 5.45 us
  local copies, waits for them, and re-layouts: 33.9 us -> 5.7 us
  between operations: 21.4 us -> 0.71 us
    psum x2 -> x0, waiting for transfers between devices: 512 us -> none  [per_device(): covariance = lax.psum(partial_cov, ('wide', 'narrow'))]
    another operation x34 -> x2, other arithmetic: 249 us -> 1.5 us  [small_table(): return jnp.stack([weight * jnp.cos(angle), weight * jnp.sin(angle)])]
    pallas_call x0 -> x6, Pallas kernels: none -> 104 us  [the longest x2 56.9 us: reduce_packed(): pl.pallas_call(reduce_kernel, name='reduce_packed', out_shape=jax.ShapeDt...]
    another operation x40 -> x0, matrix products: 37.1 us -> none  [the longest x28 26.2 us: wiener_filter(): return jax.scipy.linalg.cho_solve((factor, True), covariance)]
    mul x1 -> x2, other arithmetic: 35 us -> 0.35 us  [the longest x1 0.34 us: small_table(): return jnp.stack([weight * jnp.cos(angle), weight * jnp.sin(angle)])]
    dot_general x6 -> x1, matrix products: 33.8 us -> 5.45 us  [per_device(): jnp.einsum('srl,kslc->ksrc', masked, coeffs, preferred_element_type=F32)]
    all_to_all x1, waiting for transfers between devices: 0.01 us -> 25.2 us  [per_device(): lax.all_to_all(spectra, 'wide', split_axis=2, concat_axis=1, tiled=True)]
    another operation x35 -> x0, local copies, waits for them, and re-layouts: 23.1 us -> none  [the longest x27 22.8 us: wiener_filter(): return jax.scipy.linalg.cho_solve((factor, True), covariance)]
  transfers between devices with their start and end apart: 3 -> 1, of which waited for: 2 -> 1; matrix products, arithmetic and copies ran while one was open for 4% -> 2% of each run, Pallas kernels for 0% -> 0%
where the time goes in v1:
time: 175 us
  Pallas kernels  104 us (59%)
  waiting for transfers between devices  25.2 us (14%)
  blocking collectives  17.7 us (10%)
  starting transfers between devices  13 us (7%)
  local copies, waits for them, and re-layouts  5.7 us (3%)
  matrix products  5.45 us (3%)
  other arithmetic  2.97 us (2%)
    pallas_call x2, Pallas kernels, reduce_packed(): pl.pallas_call(reduce_kernel, name='reduce_packed', out_shape=jax.ShapeDt...  56.9 us
    all_to_all x1, waiting for transfers between devices, per_device(): lax.all_to_all(spectra, 'wide', split_axis=2, concat_axis=1, tiled=True)  25.2 us
    pallas_call x1, Pallas kernels, middle_stage(): pl.pallas_call(middle_kernel, name='middle_stage', out_shape=(jax.ShapeDt...  19.1 us
    pallas_call x1, Pallas kernels, last_stage(): pl.pallas_call(last_kernel, name='last_stage', out_shape=jax.ShapeDtypeSt...  18 us
    all_to_all x1, blocking collectives, per_device(): lax.all_to_all(sky_map, 'narrow', split_axis=0, concat_axis=1, tiled=True)  17.7 us
    all_to_all x1, starting transfers between devices, per_device(): lax.all_to_all(spectra, 'wide', split_axis=2, concat_axis=1, tiled=True)  13 us
    pallas_call x1, Pallas kernels, pixel_stage(): pl.pallas_call(pixel_kernel, name='pixel_stage', out_shape=jax.ShapeDtype...  7.16 us
    dot_general x1, matrix products, per_device(): jnp.einsum('srl,kslc->ksrc', masked, coeffs, preferred_element_type=F32)  5.45 us
  transfers between devices with their start and end apart: 1, of which 1 were waited for; matrix products, arithmetic and copies ran while one was open for 2% of the time, Pallas kernels for 0%

profile of v1, /device:TPU:1, one launch (start us, length us, event | category | flops | bytes accessed | tf_op | source)
XLA Modules:
  0.0 175.0 jit_solution(15887106482449589527)
XLA Ops:
  0.6 0.8 dynamic_slice.3
  1.4 0.1 fusion.21
  1.5 5.4 %fusion.4 = f32[2,16,64,128]{3,2,0,1:T(8,128)S(1)} fusion(bf16[2,16,1024,128]{3,2,1,0:T(8,128)(2,1)} %param.5, bf16[16,64,1024]{2,1,0:T(8,128)(2,1)} %param.6, bf16[16,1024]{1,0:T(8,128)(2,1)S(1)} %fusion.21), kind=kOutput, calls=%fused_computation.4 | convolution fusion | flops 541065216 | bytes 11567104 | tf_op jit(solution)/shard_map/srl,kslc->ksrc/dot_general | solution.py:382
  6.9 0.0 copy-start
  6.9 1.8 %copy.11 = f32[2,16,64,128]{3,0,1,2:T(2,128)} copy(f32[2,16,64,128]{3,2,0,1:T(8,128)S(1)} %fusion.4) | data formatting | bytes 2097152 | tf_op jit(solution)/shard_map/srl,kslc->ksrc/transpose | solution.py:382
  8.7 13.0 %all-to-all-start = ((f32[2,16,64,128]{3,0,1,2:T(2,128)}), f32[2,16,64,128]{3,0,1,2:T(2,128)S(1)}, u32[]{:S(2)}, u32[]{:S(2)}) async-start(f32[2,16,64,128]{3,0,1,2:T(2,128)} %copy.11), calls=%async_computation | async-start | bytes 2097152 | tf_op jit(solution)/shard_map/all_to_all | solution.py:383
  21.7 0.0 copy-done
  21.7 0.3 cosine_multiply_fusion
  22.1 0.7 pad_maximum_fusion.1.coarse_ref
  22.8 1.0 fusion.17
  23.8 0.8 pad_maximum_fusion.fine_ref
  24.6 25.2 %all-to-all-done = f32[2,16,64,128]{3,0,1,2:T(2,128)S(1)} async-done(((f32[2,16,64,128]{3,0,1,2:T(2,128)}), f32[2,16,64,128]{3,0,1,2:T(2,128)S(1)}, u32[]{:S(2)}, u32[]{:S(2)}) %all-to-all-start) | async-done | bytes 1048608 | tf_op jit(solution)/shard_map/all_to_all | solution.py:383
  49.9 1.1 copy.12
  50.9 1.0 broadcast_in_dim.28.par_ref
  51.9 7.2 %pixel_stage.1 = f32[2048,128]{1,0:T(8,128)} custom-call(f32[2,1024,128]{2,1,0:T(8,128)} %bitcast.23, f32[1024,128]{1,0:T(8,128)} %broadcast_in_dim.28.par_ref, f32[2,16,1024]{2,1,0:T(8,128)} %pad_maximum_fusion.1.coarse_ref, f32[2,64,1024]{2,1,0:T(8,128)} %pad_maximum_fusion.fine_ref), custom_call_target="tpu_custom_call" | custom-call | tf_op jit(solution)/shard_map/pixel_stage/pallas_call | solution.py:363
  59.1 17.7 %all_to_all.34 = f32[4,512,128]{2,1,0:T(8,128)S(1)} all-to-all(f32[4,512,128]{2,1,0:T(8,128)} %bitcast.24), channel_id=1, replica_groups=mesh['wide'=64,'narrow'=4] {'narrow'}, dimensions={0} | all-to-all | bytes 2097152 | tf_op jit(solution)/shard_map/all_to_all | solution.py:396
  76.7 1.1 copy_bitcast_fusion.sky_ref
  77.8 3.1 %first_stage.1 = (f32[512,512]{1,0:T(8,128)}, f32[1280,128]{1,0:T(8,128)}) custom-call(f32[512,512]{1,0:T(8,128)} %copy_bitcast_fusion.sky_ref, f32[1,512]{1,0:T(1,128)} %bitcast.27), custom_call_target="tpu_custom_call" | custom-call | tf_op jit(solution)/shard_map/first_stage/pallas_call | solution.py:287
  80.9 29.6 %reduce_packed.2.cov_ref = f32[1280,128]{1,0:T(8,128)} custom-call(f32[1280,128]{1,0:T(8,128)} %get-tuple-element.7.p_ref), custom_call_target="tpu_custom_call" | custom-call | tf_op jit(solution)/shard_map/reduce_packed/pallas_call | solution.py:156
  110.5 19.1 %middle_stage.1 = (f32[512,512]{1,0:T(8,128)}, f32[512,512]{1,0:T(8,128)}, f32[1280,128]{1,0:T(8,128)}) custom-call(f32[16]{0:T(128)} %constant.61.clone.scales_ref, f32[1280,128]{1,0:T(8,128)} %reduce_packed.2.cov_ref, f32[512,512]{1,0:T(8,128)} %get-tuple-element.8.res_ref, f32[512,512]{1,0:T(8,128)} %copy_bitcast_fusion.sky_ref, f32[1,512]{1,0:T(1,128)} %bitcast.28), custom_call_target="tpu_custom_call" | custom-call | tf_op jit(solution)/shard_map/middle_stage/pallas_call | solution.py:299
  129.7 27.3 %reduce_packed.3.cov_ref = f32[1280,128]{1,0:T(8,128)} custom-call(f32[1280,128]{1,0:T(8,128)} %get-tuple-element.9.p_ref), custom_call_target="tpu_custom_call" | custom-call | tf_op jit(solution)/shard_map/reduce_packed/pallas_call | solution.py:156
  157.0 18.0 %last_stage.1 = f32[512,512]{1,0:T(8,128)} custom-call(f32[16]{0:T(128)} %constant.61.clone.scales_ref, f32[1280,128]{1,0:T(8,128)} %reduce_packed.3.cov_ref, f32[512,512]{1,0:T(8,128)} %get-tuple-element.10.res_ref), custom_call_target="tpu_custom_call" | custom-call | tf_op jit(solution)/shard_map/last_stage/pallas_call | solution.py:314
  (3 shorter events, 0.0 us)
Async XLA Ops:
  6.9 14.8 %copy-start = (s32[1024]{0:T(1024)S(1)}, s32[1024]{0:T(1024)}, u32[]{:S(2)}) copy-start(s32[1024]{0:T(1024)} %param.7) | copy-start | bytes 12292
  8.7 41.1 %all-to-all-start = ((f32[2,16,64,128]{3,0,1,2:T(2,128)}), f32[2,16,64,128]{3,0,1,2:T(2,128)S(1)}, u32[]{:S(2)}, u32[]{:S(2)}) async-start(f32[2,16,64,128]{3,0,1,2:T(2,128)} %copy.11), calls=%async_computation | async-start | bytes 2097152 | tf_op jit(solution)/shard_map/all_to_all | solution.py:383

commit v2 on v1

--- a/solution.py
+++ b/solution.py
@@ -194,9 +194,10 @@
             at += 128
 
 
-def first_kernel(sky_ref, thr_ref, res_ref, cov_ref, left, right):
+def first_kernel(parts_ref, thr_ref, sky_ref, res_ref, cov_ref, left, right):
     thr = thr_ref[...]
-    sky = sky_ref[...]
+    sky = jnp.concatenate([parts_ref[i] for i in range(NB)], axis=1)
+    sky_ref[...] = sky
     res = sky - (sky - jnp.minimum(jnp.maximum(sky, -thr), thr))
     res_ref[...] = res
     put_cov(res, cov_ref, left, right)
@@ -282,16 +283,20 @@
     ]
 
 
-def first_stage(sky, thr):
-    pix = sky.shape[0]
+def first_stage(parts, thr):
+    pix = parts.shape[1]
     return pl.pallas_call(
         first_kernel,
         name="first_stage",
-        out_shape=(jax.ShapeDtypeStruct((pix, NCH), F32), jax.ShapeDtypeStruct((ROWS, 128), F32)),
+        out_shape=(
+            jax.ShapeDtypeStruct((pix, NCH), F32),
+            jax.ShapeDtypeStruct((pix, NCH), F32),
+            jax.ShapeDtypeStruct((ROWS, 128), F32),
+        ),
         in_specs=[VM, VM],
-        out_specs=(VM, VM),
+        out_specs=(VM, VM, VM),
         scratch_shapes=[pltpu.VMEM((3 * pix, NCH), BF16), pltpu.VMEM((3 * pix, NCH), BF16)],
-    )(sky, thr)
+    )(parts, thr)
 
 
 def middle_stage(scales, cov, res, sky, thr):
@@ -323,80 +328,199 @@
 
 SB = 64
 HP = NPIX // 2
-STEP = 4
-
-
-def pixel_kernel(spec_ref, par_ref, coarse_ref, fine_ref, sky_ref, rhs):
-    ns = spec_ref.shape[1]
-    even = par_ref[...]
-    for k in range(2):
-        value = spec_ref[k]
-        for p, part in enumerate((value * even, value * (1.0 - even))):
-            hi, lo = split(part)
-            rhs[k * ns : (k + 1) * ns, p * 128 : (p + 1) * 128] = hi
-            rhs[k * ns : (k + 1) * ns, 256 + p * 128 : 256 + (p + 1) * 128] = lo
-
-    def step(i, carry):
-        tops = []
-        for q in range(STEP):
-            a = i * STEP + q
-            ca = coarse_ref[0, pl.ds(a, 1), :]
-            sa = coarse_ref[1, pl.ds(a, 1), :]
-            cb, sb = fine_ref[0], fine_ref[1]
-            tops.append(jnp.concatenate([ca * cb - sa * sb, -(sa * cb + ca * sb)], axis=1))
-        table = jnp.concatenate(tops, axis=0)
-        hi, lo = split(table)
-        top = dot(hi, rhs[...])
-        low = dot(lo, rhs[:, 0:256])
-        e = top[:, 0:128] + top[:, 256:384] + low[:, 0:128]
-        o = top[:, 128:256] + top[:, 384:512] + low[:, 128:256]
-        j = pl.multiple_of(i * (STEP * SB), STEP * SB)
-        sky_ref[pl.ds(j, STEP * SB), :] = e + o
-        sky_ref[pl.ds(j + HP, STEP * SB), :] = e - o
+WIDE = 2 * X * Z
+GROUPS = 2
+SUBS = 2
+
+
+def front_kernel(
+    ord_ref, row_ref, leg_hbm, co_hbm, out_ref,
+    leg_v, co_v, sp, rb, th, tl, trig_a, trig_b, par, rhs, stage,
+    ls, s1, r1, s2, r2,
+):
+    slots, cycles, degrees = leg_v.shape
+    total = WIDE * slots
+    gs = slots // GROUPS
+    w = lax.axis_index("wide")
+    y = lax.axis_index("narrow")
+    core = lax.rem(w, 2)
+    x = lax.rem(w // 2, X)
+    z = w // (2 * X)
+
+    offsets = [(dz, dx, dc) for dz in range(Z) for dx in range(X) for dc in range(2)][1:]
+    offsets.sort(key=lambda o: (-min(o[0], Z - o[0]) - min(o[1], X - o[1]), o[1], o[2], o[0]))
+
+    def at(sign, o):
+        dz, dx, dc = o
+        pz = lax.rem(z + (dz if sign > 0 else Z - dz), Z)
+        px = lax.rem(x + (dx if sign > 0 else X - dx), X)
+        return pz * 2 * X + px * 2 + (lax.rem(core + dc, 2))
+
+    def ring(d):
+        return (w, lax.rem(y + d, Y))
+
+    def loads(s):
+        return [pltpu.make_async_copy(leg_hbm.at[s], leg_v.at[s], ls.at[0, s])] + [
+            pltpu.make_async_copy(co_hbm.at[k, s], co_v.at[s, :, k * 128 : (k + 1) * 128], ls.at[1 + k, s])
+            for k in range(2)
+        ]
+
+    pending = [loads(s) for s in range(slots)]
+    for copies in pending:
+        for copy in copies:
+            copy.start()
+
+    barrier = pltpu.get_barrier_semaphore()
+    for o in offsets:
+        pl.semaphore_signal(barrier, inc=1, device_id=(at(1, o), y), device_id_type=MESH)
+    for d in range(1, Y):
+        pl.semaphore_signal(barrier, inc=1, device_id=ring(d), device_id_type=MESH)
+
+    def remote(src, dst, send, recv, peer):
+        return pltpu.make_async_remote_copy(
+            src_ref=src, dst_ref=dst, send_sem=send, recv_sem=recv, device_id=peer, device_id_type=MESH
+        )
+
+    degree = lax.broadcasted_iota(jnp.int32, (cycles, degrees), 1)
+    sends = {}
+    for g in range(GROUPS):
+        for t in range(gs):
+            s = g * gs + t
+            for copy in pending[s]:
+                copy.wait()
+            order = ord_ref[w * slots + s]
+            table = jnp.where(degree >= order, leg_v[s].astype(F32), 0.0).astype(BF16)
+            value = dot(table, co_v[s])
+            for k in range(2):
+                sp[g, pl.ds(k * gs + t, cycles, stride=2 * gs), :] = value[:, k * 128 : (k + 1) * 128]
+        if g == 0:
+            pl.semaphore_wait(barrier, len(offsets) + Y - 1)
+        for r, o in enumerate(offsets):
+            to = at(1, o)
+            sends[g, r] = remote(
+                sp.at[g, pl.ds(pl.multiple_of(to * 2 * gs, 8), 2 * gs), :], rb.at[g, w], s1.at[g, r], r1.at[g, r], (to, y)
+            )
+            sends[g, r].start()
+
+    orders = row_ref[...]
+    weights = jnp.where(orders == 0, 1.0, 2.0).astype(F32)
+
+    def trig(ref, steps, stride, weight):
+        turn = orders * (lax.broadcasted_iota(jnp.int32, (steps, total), 0) * stride)
+        angle = jnp.bitwise_and(turn, NPIX - 1).astype(F32) * (2.0 * math.pi / NPIX)
+        ref[0] = weight * jnp.cos(angle)
+        ref[1] = weight * jnp.sin(angle)
+
+    trig(trig_a, HP // SB, SB, weights)
+    trig(trig_b, SB, 1, 1.0)
+    even = (1 - jnp.bitwise_and(orders, 1)).astype(F32)
+    for b in range(total // 128):
+        par[b * 128 : (b + 1) * 128, :] = jnp.broadcast_to(even[:, b * 128 : (b + 1) * 128], (128, 128)).T
+
+    def fill(a, carry):
+        rows = pl.ds(pl.multiple_of(a * SB, SB), SB)
+        ca = trig_a[0, pl.ds(a, 1), :]
+        sa = trig_a[1, pl.ds(a, 1), :]
+        cb, sb = trig_b[0], trig_b[1]
+        for k, value in enumerate((ca * cb - sa * sb, -(sa * cb + ca * sb))):
+            hi, lo = split(value)
+            th[rows, k * total : (k + 1) * total] = hi
+            tl[rows, k * total : (k + 1) * total] = lo
         return carry
 
-    lax.fori_loop(0, HP // (SB * STEP), step, 0)
-
-
-def pixel_stage(spec, parity, coarse, fine):
-    ns = spec.shape[1]
+    lax.fori_loop(0, HP // SB, fill, 0)
+
+    def prepare(src):
+        rows = pl.ds(pl.multiple_of(src * slots, slots), slots)
+        evens = par[rows, :]
+        for k in range(2):
+            value = jnp.concatenate([rb[g, src, k * gs : (k + 1) * gs, :] for g in range(GROUPS)], axis=0)
+            own = value * evens
+            at_k = pl.ds(pl.multiple_of(k * total + src * slots, slots), slots)
+            for p, part in enumerate((own, value - own)):
+                hi, lo = split(part)
+                rhs[at_k, p * 128 : (p + 1) * 128] = hi
+                rhs[at_k, 256 + p * 128 : 256 + (p + 1) * 128] = lo
+
+    for g in range(GROUPS):
+        rb[g, w] = sp[g, pl.ds(pl.multiple_of(w * 2 * gs, 8), 2 * gs), :]
+    prepare(w)
+    for r, o in enumerate(offsets):
+        for g in range(GROUPS):
+            sends[g, r].wait_recv()
+        prepare(at(-1, o))
+
+    width = NPIX // Y
+    sub = width // SUBS
+    outs = {}
+    for d in (2, 1):
+        first = lax.rem(y + d, Y)
+        sign = jnp.where(first < Y // 2, 1.0, -1.0).astype(F32)
+        start = lax.rem(first, Y // 2) * width
+        for b in range(SUBS):
+            rows = pl.ds(pl.multiple_of(start + b * sub, sub), sub)
+            top = dot(th[rows, :], rhs[...])
+            low = dot(tl[rows, :], rhs[:, 0:256])
+            e = top[:, 0:128] + top[:, 256:384] + low[:, 0:128]
+            o = sign * (top[:, 128:256] + top[:, 384:512] + low[:, 128:256])
+            for q, value in ((d, e + o), ((d + 2) % Y, e - o)):
+                mine = slice(b * sub, (b + 1) * sub)
+                if q == 0:
+                    out_ref[y, mine, :] = value
+                else:
+                    stage[q - 1, mine, :] = value
+                    outs[q, b] = remote(
+                        stage.at[q - 1, mine, :], out_ref.at[y, mine, :], s2.at[q, b], r2.at[q, b], ring(q)
+                    )
+                    outs[q, b].start()
+    for copy in outs.values():
+        copy.wait_recv()
+    for copy in outs.values():
+        copy.wait_send()
+    for copy in sends.values():
+        copy.wait_send()
+
+
+def front_stage(order_table, legendre, coeffs):
+    slots, cycles, degrees = legendre.shape
+    total = WIDE * slots
+    gs = slots // GROUPS
+    width = NPIX // Y
+    dma = pltpu.SemaphoreType.DMA
+    hbm = pl.BlockSpec(memory_space=pl.ANY)
     return pl.pallas_call(
-        pixel_kernel,
-        name="pixel_stage",
-        out_shape=jax.ShapeDtypeStruct((NPIX, spec.shape[2]), F32),
-        in_specs=[VM, VM, VM, VM],
+        front_kernel,
+        name="front_stage",
+        out_shape=jax.ShapeDtypeStruct((Y, width, 128), F32),
+        in_specs=[SM, VM, hbm, hbm],
         out_specs=VM,
-        scratch_shapes=[pltpu.VMEM((2 * ns, 512), BF16)],
-    )(spec, parity, coarse, fine)
+        scratch_shapes=[
+            pltpu.VMEM((slots, cycles, degrees), BF16),
+            pltpu.VMEM((slots, degrees, 256), BF16),
+            pltpu.VMEM((GROUPS, cycles * 2 * gs, 128), F32),
+            pltpu.VMEM((GROUPS, WIDE, 2 * gs, 128), F32),
+            pltpu.VMEM((HP, 2 * total), BF16),
+            pltpu.VMEM((HP, 2 * total), BF16),
+            pltpu.VMEM((2, HP // SB, total), F32),
+            pltpu.VMEM((2, SB, total), F32),
+            pltpu.VMEM((total, 128), F32),
+            pltpu.VMEM((2 * total, 512), BF16),
+            pltpu.VMEM((Y - 1, width, 128), F32),
+            dma((3, slots)),
+            dma((GROUPS, WIDE)),
+            dma((GROUPS, WIDE)),
+            dma((Y, SUBS)),
+            dma((Y, SUBS)),
+        ],
+        compiler_params=pltpu.CompilerParams(collective_id=1, has_side_effects=True),
+    )(order_table, order_table[None, :], legendre, coeffs)
 
 
 def per_device(coeffs, legendre, order_table, thresholds):
-    slot_count = legendre.shape[0]
-    degrees = legendre.shape[2]
-    first_slot = lax.axis_index("wide") * slot_count
-    own_orders = lax.dynamic_slice_in_dim(order_table, first_slot, slot_count)
-    degree_mask = (
-        lax.broadcasted_iota(jnp.int32, (slot_count, degrees), 1) >= own_orders[:, None]
-    ).astype(legendre.dtype)
-    masked = legendre * degree_mask[:, None, :]
-    spectra = jnp.einsum("srl,kslc->ksrc", masked, coeffs, preferred_element_type=F32)
-    spec = lax.all_to_all(spectra, "wide", split_axis=2, concat_axis=1, tiled=True)[:, :, 0, :]
-
-    weights = jnp.where(order_table == 0, 1.0, 2.0).astype(F32)[None, :]
-
-    def small_table(steps, stride, weight):
-        at = lax.broadcasted_iota(jnp.int32, (steps, 1), 0) * stride
-        angle = (order_table[None, :] * at % NPIX).astype(F32) * (2.0 * math.pi / NPIX)
-        return jnp.stack([weight * jnp.cos(angle), weight * jnp.sin(angle)])
-
-    coarse = small_table(HP // SB, SB, weights)
-    fine = small_table(SB, 1, 1.0)
-    parity = jnp.broadcast_to((1 - order_table % 2).astype(F32)[:, None], (order_table.shape[0], 128))
-    sky_map = pixel_stage(spec, parity, coarse, fine)
-    sky = lax.all_to_all(sky_map, "narrow", split_axis=0, concat_axis=1, tiled=True)
+    parts = front_stage(order_table, legendre, coeffs)
     thr = thresholds[None, :]
     scales = jnp.asarray(SCALES + [0.0] * (16 - len(SCALES)), F32)
-    res, cov = first_stage(sky, thr)
+    sky, res, cov = first_stage(parts, thr)
     sparse, res, cov = middle_stage(scales, reduce_packed(cov), res, sky, thr)
     low = last_stage(scales, reduce_packed(cov), res)
     return low[None], sparse[None]

time: 175 us -> 154 us (0.88)
  Pallas kernels: 104 us -> 153 us
  waiting for transfers between devices: 25.2 us -> 0 us
  blocking collectives: 17.7 us -> 0 us
  starting transfers between devices: 13 us -> 0 us
  local copies, waits for them, and re-layouts: 5.7 us -> 0 us
  matrix products: 5.45 us -> 0 us
  other arithmetic: 2.97 us -> 0 us
    pallas_call x1, Pallas kernels: 7.16 us -> 57.6 us  [front_stage(): pl.pallas_call(front_kernel, name='front_stage', out_shape=jax.ShapeDtype...]
    all_to_all x1 -> x0, waiting for transfers between devices: 25.2 us -> none  [per_device(): lax.all_to_all(spectra, 'wide', split_axis=2, concat_axis=1, tiled=True)]
    all_to_all x1 -> x0, blocking collectives: 17.7 us -> none  [per_device(): lax.all_to_all(sky_map, 'narrow', split_axis=0, concat_axis=1, tiled=True)]
    all_to_all x1 -> x0, starting transfers between devices: 13 us -> none  [per_device(): lax.all_to_all(spectra, 'wide', split_axis=2, concat_axis=1, tiled=True)]
    dot_general x1 -> x0, matrix products: 5.45 us -> none  [per_device(): jnp.einsum('srl,kslc->ksrc', masked, coeffs, preferred_element_type=F32)]
    all_to_all x2 -> x0, local copies, waits for them, and re-layouts: 2.16 us -> none  [the longest x1 1.11 us: per_device(): lax.all_to_all(sky_map, 'narrow', split_axis=0, concat_axis=1, tiled=True)]
    transpose x1 -> x0, local copies, waits for them, and re-layouts: 1.78 us -> none  [per_device(): jnp.einsum('srl,kslc->ksrc', masked, coeffs, preferred_element_type=F32)]
  transfers between devices with their start and end apart: 1 -> 0, of which waited for: 1 -> 0; matrix products, arithmetic and copies ran while one was open for 2% -> 0% of each run, Pallas kernels for 0% -> 0%
where the time goes in v2:
time: 154 us
  Pallas kernels  153 us (99%)
    pallas_call x1, Pallas kernels, front_stage(): pl.pallas_call(front_kernel, name='front_stage', out_shape=jax.ShapeDtype...  57.6 us
    pallas_call x2, Pallas kernels, reduce_packed(): pl.pallas_call(reduce_kernel, name='reduce_packed', out_shape=jax.ShapeDt...  55.5 us
    pallas_call x1, Pallas kernels, middle_stage(): pl.pallas_call(middle_kernel, name='middle_stage', out_shape=(jax.ShapeDt...  19.3 us
    pallas_call x1, Pallas kernels, last_stage(): pl.pallas_call(last_kernel, name='last_stage', out_shape=jax.ShapeDtypeSt...  17.8 us
    pallas_call x1, Pallas kernels, first_stage(): pl.pallas_call(first_kernel, name='first_stage', out_shape=(jax.ShapeDtyp...  3.13 us

profile of v2, /device:TPU:1, one launch (start us, length us, event | category | flops | bytes accessed | tf_op | source)
XLA Modules:
  0.0 154.0 jit_solution(3850966906406069416)
XLA Ops:
  0.6 57.6 %front_stage.1.parts_ref = f32[4,512,128]{2,1,0:T(8,128)} custom-call(s32[1024]{0:T(1024)} %ord_ref.1, s32[1,1024]{1,0:T(1,128)} %bitcast.5, bf16[16,64,1024]{2,1,0:T(8,128)(2,1)} %leg_hbm.1, bf16[2,16,1024,128]{3,2,1,0:T(8,128)(2,1)} %co_hbm.1), custom_call_target="tpu_custom_call" | custom-call | tf_op jit(solution)/shard_map/front_stage/pallas_call | solution.py:491
  58.2 3.1 %first_stage.1 = (f32[512,512]{1,0:T(8,128)}, f32[512,512]{1,0:T(8,128)}, f32[1280,128]{1,0:T(8,128)}) custom-call(f32[4,512,128]{2,1,0:T(8,128)} %front_stage.1.parts_ref, f32[1,512]{1,0:T(1,128)} %bitcast.6), custom_call_target="tpu_custom_call" | custom-call | tf_op jit(solution)/shard_map/first_stage/pallas_call | solution.py:288
  61.4 28.3 %reduce_packed.2.cov_ref = f32[1280,128]{1,0:T(8,128)} custom-call(f32[1280,128]{1,0:T(8,128)} %get-tuple-element.8.p_ref), custom_call_target="tpu_custom_call" | custom-call | tf_op jit(solution)/shard_map/reduce_packed/pallas_call | solution.py:156
  89.7 19.3 %middle_stage.1 = (f32[512,512]{1,0:T(8,128)}, f32[512,512]{1,0:T(8,128)}, f32[1280,128]{1,0:T(8,128)}) custom-call(f32[16]{0:T(128)} %constant.2.clone.scales_ref, f32[1280,128]{1,0:T(8,128)} %reduce_packed.2.cov_ref, f32[512,512]{1,0:T(8,128)} %get-tuple-element.9.res_ref, f32[512,512]{1,0:T(8,128)} %get-tuple-element.10.sky_ref, f32[1,512]{1,0:T(1,128)} %bitcast.7), custom_call_target="tpu_custom_call" | custom-call | tf_op jit(solution)/shard_map/middle_stage/pallas_call | solution.py:304
  109.0 27.2 %reduce_packed.3.cov_ref = f32[1280,128]{1,0:T(8,128)} custom-call(f32[1280,128]{1,0:T(8,128)} %get-tuple-element.11.p_ref), custom_call_target="tpu_custom_call" | custom-call | tf_op jit(solution)/shard_map/reduce_packed/pallas_call | solution.py:156
  136.2 17.8 %last_stage.1 = f32[512,512]{1,0:T(8,128)} custom-call(f32[16]{0:T(128)} %constant.2.clone.scales_ref, f32[1280,128]{1,0:T(8,128)} %reduce_packed.3.cov_ref, f32[512,512]{1,0:T(8,128)} %get-tuple-element.12.res_ref), custom_call_target="tpu_custom_call" | custom-call | tf_op jit(solution)/shard_map/last_stage/pallas_call | solution.py:319

commit v3 on v2

--- a/solution.py
+++ b/solution.py
@@ -63,7 +63,7 @@
     ref[2 * n : 3 * n, :] = lo
 
 
-def reduce_kernel(p_ref, out_ref, b1, acc1, b2, acc2, b3, acc3, s1, r1, s2, r2, s3, r3, s4, r4, s5, r5):
+def reduce_peers():
     w = lax.axis_index("wide")
     y = lax.axis_index("narrow")
     core = lax.rem(w, 2)
@@ -80,11 +80,19 @@
     def deep(d):
         return (lax.rem(z + d, Z) * 2 * X + x * 2 + core, y)
 
+    return x, y, core, other, partner, plane, deep
+
+
+def greet():
+    _, _, _, _, partner, plane, deep = reduce_peers()
     barrier = pltpu.get_barrier_semaphore()
-    peers = [partner] + [plane(k)[0] for k in range(1, X * Y)] + [deep(d) for d in range(1, Z)]
-    for peer in peers:
+    for peer in [partner] + [plane(k)[0] for k in range(1, X * Y)] + [deep(d) for d in range(1, Z)]:
         pl.semaphore_signal(barrier, inc=1, device_id=peer, device_id_type=MESH)
-    pl.semaphore_wait(barrier, len(peers))
+
+
+def reduce_all(p_ref, out_ref, b1, acc1, b2, acc2, b3, acc3, s1, r1, s2, r2, s3, r3, s4, r4, s5, r5):
+    x, y, core, other, partner, plane, deep = reduce_peers()
+    pl.semaphore_wait(pltpu.get_barrier_semaphore(), X * Y + Z - 1)
 
     order = sorted(range(X * Y), key=lambda k: -(min(k // Y, X - k // Y) + min(k % Y, Y - k % Y)))
 
@@ -150,16 +158,12 @@
         third[d].wait_send()
 
 
-def reduce_packed(packed):
+def reduce_scratch():
     n = X * Y
     dma = pltpu.SemaphoreType.DMA
-    return pl.pallas_call(
-        reduce_kernel,
-        name="reduce_packed",
-        out_shape=jax.ShapeDtypeStruct((ROWS, 128), F32),
-        in_specs=[pl.BlockSpec(memory_space=pltpu.VMEM)],
-        out_specs=pl.BlockSpec(memory_space=pltpu.VMEM),
-        scratch_shapes=[
+    return (
+        [
+            pltpu.VMEM((ROWS, 128), F32),
             pltpu.VMEM((n, CHUNK, 128), F32),
             pltpu.VMEM((n, CHUNK, 128), F32),
             pltpu.VMEM((n, CHUNK, 128), F32),
@@ -169,9 +173,8 @@
         ]
         + [dma((n,))] * 4
         + [dma((Z,))] * 2
-        + [dma((n,))] * 4,
-        compiler_params=pltpu.CompilerParams(collective_id=0, has_side_effects=True),
-    )(packed)
+        + [dma((n,))] * 4
+    )
 
 
 def put_cov(res, cov_ref, left, right):
@@ -194,13 +197,15 @@
             at += 128
 
 
-def first_kernel(parts_ref, thr_ref, sky_ref, res_ref, cov_ref, left, right):
+def first_kernel(parts_ref, thr_ref, sky_ref, res_ref, cov_ref, left, right, part_ref, *reduce_refs):
+    greet()
     thr = thr_ref[...]
     sky = jnp.concatenate([parts_ref[i] for i in range(NB)], axis=1)
     sky_ref[...] = sky
     res = sky - (sky - jnp.minimum(jnp.maximum(sky, -thr), thr))
     res_ref[...] = res
-    put_cov(res, cov_ref, left, right)
+    put_cov(res, part_ref, left, right)
+    reduce_all(part_ref, cov_ref, *reduce_refs)
 
 
 def put_inverse(cov_ref, scales_ref, a_ref, x_ref, a3, xl, xr):
@@ -252,7 +257,11 @@
     return res - dot(xl[...], xr[...])
 
 
-def middle_kernel(scales_ref, cov_ref, res_ref, sky_ref, thr_ref, sparse_ref, res2_ref, cov2_ref, a_ref, x_ref, a3, xl, xr):
+def middle_kernel(
+    scales_ref, cov_ref, res_ref, sky_ref, thr_ref, sparse_ref, res2_ref, cov2_ref,
+    a_ref, x_ref, a3, xl, xr, part_ref, *reduce_refs,
+):
+    greet()
     put_inverse(cov_ref, scales_ref, a_ref, x_ref, a3, xl, xr)
     thr = thr_ref[...]
     sky = sky_ref[...]
@@ -261,12 +270,16 @@
     sparse_ref[...] = sparse
     res = sky - sparse
     res2_ref[...] = res
-    put_cov(res, cov2_ref, a3, xr)
-
-
-def last_kernel(scales_ref, cov_ref, res_ref, low_ref, a_ref, x_ref, a3, xl, xr):
+    put_cov(res, part_ref, a3, xr)
+    reduce_all(part_ref, cov2_ref, *reduce_refs)
+
+
+def last_kernel(scales_ref, cov_ref, res_ref, sparse_ref, low_ref, out_ref, a_ref, x_ref, a3, xl, xr, sem):
+    copy = pltpu.make_async_copy(sparse_ref, out_ref, sem)
+    copy.start()
     put_inverse(cov_ref, scales_ref, a_ref, x_ref, a3, xl, xr)
     low_ref[...] = low_of(res_ref, xl, xr)
+    copy.wait()
 
 
 VM = pl.BlockSpec(memory_space=pltpu.VMEM)
@@ -295,7 +308,8 @@
         ),
         in_specs=[VM, VM],
         out_specs=(VM, VM, VM),
-        scratch_shapes=[pltpu.VMEM((3 * pix, NCH), BF16), pltpu.VMEM((3 * pix, NCH), BF16)],
+        scratch_shapes=[pltpu.VMEM((3 * pix, NCH), BF16), pltpu.VMEM((3 * pix, NCH), BF16)] + reduce_scratch(),
+        compiler_params=pltpu.CompilerParams(collective_id=2, has_side_effects=True),
     )(parts, thr)
 
 
@@ -311,19 +325,20 @@
         ),
         in_specs=[SM, VM, VM, VM, VM],
         out_specs=(VM, VM, VM),
-        scratch_shapes=inverse_scratch(),
+        scratch_shapes=inverse_scratch() + reduce_scratch(),
+        compiler_params=pltpu.CompilerParams(collective_id=3, has_side_effects=True),
     )(scales, cov, res, sky, thr)
 
 
-def last_stage(scales, cov, res):
+def last_stage(scales, cov, res, sparse):
     return pl.pallas_call(
         last_kernel,
         name="last_stage",
-        out_shape=jax.ShapeDtypeStruct(res.shape, F32),
-        in_specs=[SM, VM, VM],
-        out_specs=VM,
-        scratch_shapes=inverse_scratch(),
-    )(scales, cov, res)
+        out_shape=(jax.ShapeDtypeStruct(res.shape, F32), jax.ShapeDtypeStruct(res.shape, F32)),
+        in_specs=[SM, VM, VM, VM],
+        out_specs=(VM, pl.BlockSpec(memory_space=pl.ANY)),
+        scratch_shapes=inverse_scratch() + [pltpu.SemaphoreType.DMA],
+    )(scales, cov, res, sparse)
 
 
 SB = 64
@@ -521,8 +536,8 @@
     thr = thresholds[None, :]
     scales = jnp.asarray(SCALES + [0.0] * (16 - len(SCALES)), F32)
     sky, res, cov = first_stage(parts, thr)
-    sparse, res, cov = middle_stage(scales, reduce_packed(cov), res, sky, thr)
-    low = last_stage(scales, reduce_packed(cov), res)
+    sparse, res, cov = middle_stage(scales, cov, res, sky, thr)
+    low, sparse = last_stage(scales, cov, res, sparse)
     return low[None], sparse[None]
 
 

time: 154 us -> 148 us (0.961)
  Pallas kernels: 153 us -> 147 us
    pallas_call x3 -> x1, Pallas kernels: 73.3 us -> 18.1 us  [last_stage(): pl.pallas_call(last_kernel, name='last_stage', out_shape=(jax.ShapeDtypeS...]
    pallas_call x1, Pallas kernels: 3.13 us -> 29.2 us  [first_stage(): pl.pallas_call(first_kernel, name='first_stage', out_shape=(jax.ShapeDtyp...]
    pallas_call x1, Pallas kernels: 19.3 us -> 42.5 us  [middle_stage(): pl.pallas_call(middle_kernel, name='middle_stage', out_shape=(jax.ShapeDt...]
where the time goes in v3:
time: 148 us
  Pallas kernels  147 us (99%)
    pallas_call x1, Pallas kernels, front_stage(): pl.pallas_call(front_kernel, name='front_stage', out_shape=jax.ShapeDtype...  57.6 us
    pallas_call x1, Pallas kernels, middle_stage(): pl.pallas_call(middle_kernel, name='middle_stage', out_shape=(jax.ShapeDt...  42.5 us
    pallas_call x1, Pallas kernels, first_stage(): pl.pallas_call(first_kernel, name='first_stage', out_shape=(jax.ShapeDtyp...  29.2 us
    pallas_call x1, Pallas kernels, last_stage(): pl.pallas_call(last_kernel, name='last_stage', out_shape=(jax.ShapeDtypeS...  18.1 us

profile of v3, /device:TPU:1, one launch (start us, length us, event | category | flops | bytes accessed | tf_op | source)
XLA Modules:
  0.0 148.2 jit_solution(17582630180722815027)
XLA Ops:
  0.6 57.6 %front_stage.1.parts_ref = f32[4,512,128]{2,1,0:T(8,128)} custom-call(s32[1024]{0:T(1024)} %ord_ref.1, s32[1,1024]{1,0:T(1,128)} %bitcast.4, bf16[16,64,1024]{2,1,0:T(8,128)(2,1)} %leg_hbm.1, bf16[2,16,1024,128]{3,2,1,0:T(8,128)(2,1)} %co_hbm.1), custom_call_target="tpu_custom_call" | custom-call | tf_op jit(solution)/shard_map/front_stage/pallas_call | solution.py:506
  58.2 29.2 %first_stage.1 = (f32[512,512]{1,0:T(8,128)}, f32[512,512]{1,0:T(8,128)}, f32[1280,128]{1,0:T(8,128)}) custom-call(f32[4,512,128]{2,1,0:T(8,128)} %front_stage.1.parts_ref, f32[1,512]{1,0:T(1,128)} %bitcast.5), custom_call_target="tpu_custom_call" | custom-call | tf_op jit(solution)/shard_map/first_stage/pallas_call | solution.py:301
  87.4 42.5 %middle_stage.1 = (f32[512,512]{1,0:T(8,128)}, f32[512,512]{1,0:T(8,128)}, f32[1280,128]{1,0:T(8,128)}) custom-call(f32[16]{0:T(128)} %constant.2.clone.scales_ref, f32[1280,128]{1,0:T(8,128)} %get-tuple-element.10.cov_ref, f32[512,512]{1,0:T(8,128)} %get-tuple-element.11.res_ref, f32[512,512]{1,0:T(8,128)} %get-tuple-element.12.sky_ref, f32[1,512]{1,0:T(1,128)} %bitcast.6), custom_call_target="tpu_custom_call" | custom-call | tf_op jit(solution)/shard_map/middle_stage/pallas_call | solution.py:318
  129.9 18.1 %last_stage.1 = (f32[512,512]{1,0:T(8,128)}, f32[512,512]{1,0:T(8,128)}) custom-call(f32[16]{0:T(128)} %constant.2.clone.scales_ref, f32[1280,128]{1,0:T(8,128)} %get-tuple-element.13.cov_ref, f32[512,512]{1,0:T(8,128)} %get-tuple-element.14.res_ref, f32[512,512]{1,0:T(8,128)} %get-tuple-element.15.sparse_ref), custom_call_target="tpu_custom_call" | custom-call | tf_op jit(solution)/shard_map/last_stage/pallas_call | solution.py:334

commit v4 on v3

--- a/solution.py
+++ b/solution.py
@@ -29,7 +29,7 @@
 def newton_scales():
     delta = (KAPPA - 1.0) / (KAPPA + 1.0)
     scales = []
-    while delta > 1e-4:
+    while delta > 1e-2:
         scales.append(2.0 / (2.0 - delta * delta))
         delta = delta * delta / (2.0 - delta * delta)
     return scales
@@ -197,7 +197,14 @@
             at += 128
 
 
-def first_kernel(parts_ref, thr_ref, sky_ref, res_ref, cov_ref, left, right, part_ref, *reduce_refs):
+def moves(pairs, sems):
+    copies = [pltpu.make_async_copy(src, dst, sems.at[i]) for i, (src, dst) in enumerate(pairs)]
+    for copy in copies:
+        copy.start()
+    return copies
+
+
+def first_kernel(parts_ref, thr_ref, sky_out, res_out, cov_ref, left, right, sky_ref, res_ref, sems, part_ref, *reduce_refs):
     greet()
     thr = thr_ref[...]
     sky = jnp.concatenate([parts_ref[i] for i in range(NB)], axis=1)
@@ -205,10 +212,13 @@
     res = sky - (sky - jnp.minimum(jnp.maximum(sky, -thr), thr))
     res_ref[...] = res
     put_cov(res, part_ref, left, right)
+    outs = moves(((sky_ref, sky_out), (res_ref, res_out)), sems)
     reduce_all(part_ref, cov_ref, *reduce_refs)
-
-
-def put_inverse(cov_ref, scales_ref, a_ref, x_ref, a3, xl, xr):
+    for copy in outs:
+        copy.wait()
+
+
+def put_inverse(cov_ref, scales_ref, a_ref, x_ref, a3, xl, xr, wl):
     eye = (lax.broadcasted_iota(jnp.int32, (128, 128), 0) == lax.broadcasted_iota(jnp.int32, (128, 128), 1)).astype(F32)
     diag = jnp.zeros((128, 128), F32)
     for idx, (i, j) in enumerate(PAIRS):
@@ -236,8 +246,8 @@
 
     def step(k, carry):
         wa = dot(xl[...], a3[...])
-        put_left(xl, wa)
-        x = scales_ref[k] * (2.0 * x_ref[...] - dot(xl[...], xr[...]))
+        put_left(wl, wa)
+        x = scales_ref[k] * (2.0 * x_ref[...] - dot(wl[...], xr[...]))
         x_ref[...] = x
         put_left(xl, x)
         put_right(xr, x)
@@ -246,9 +256,9 @@
     lax.fori_loop(1, len(SCALES), step, 0)
     x = x_ref[...]
     rest = full_eye - jnp.dot(x, a_ref[...], preferred_element_type=F32, precision=lax.Precision.HIGHEST)
-    x = x + dot(rest.astype(BF16), xr[0:NCH, :])
-    x_ref[...] = x
-    put_right(xr, x)
+    put_left(wl, rest)
+    put_right(a3, x + dot(wl[:, 0:NCH], xr[0:NCH, :]))
+    put_right(xr, x + dot(wl[...], a3[...]))
 
 
 def low_of(res_ref, xl, xr):
@@ -258,11 +268,14 @@
 
 
 def middle_kernel(
-    scales_ref, cov_ref, res_ref, sky_ref, thr_ref, sparse_ref, res2_ref, cov2_ref,
-    a_ref, x_ref, a3, xl, xr, part_ref, *reduce_refs,
+    scales_ref, cov_ref, res_in, sky_in, thr_ref, sparse_out, res2_out, cov2_ref,
+    a_ref, x_ref, a3, xl, xr, wl, res_ref, sky_ref, sparse_ref, res2_ref, in_sems, out_sems, part_ref, *reduce_refs,
 ):
+    ins = moves(((res_in, res_ref), (sky_in, sky_ref)), in_sems)
     greet()
-    put_inverse(cov_ref, scales_ref, a_ref, x_ref, a3, xl, xr)
+    put_inverse(cov_ref, scales_ref, a_ref, x_ref, a3, xl, xr, wl)
+    for copy in ins:
+        copy.wait()
     thr = thr_ref[...]
     sky = sky_ref[...]
     v = sky - low_of(res_ref, xl, xr)
@@ -271,19 +284,28 @@
     res = sky - sparse
     res2_ref[...] = res
     put_cov(res, part_ref, a3, xr)
+    outs = moves(((sparse_ref, sparse_out), (res2_ref, res2_out)), out_sems)
     reduce_all(part_ref, cov2_ref, *reduce_refs)
-
-
-def last_kernel(scales_ref, cov_ref, res_ref, sparse_ref, low_ref, out_ref, a_ref, x_ref, a3, xl, xr, sem):
-    copy = pltpu.make_async_copy(sparse_ref, out_ref, sem)
-    copy.start()
-    put_inverse(cov_ref, scales_ref, a_ref, x_ref, a3, xl, xr)
+    for copy in outs:
+        copy.wait()
+
+
+def last_kernel(
+    scales_ref, cov_ref, res_in, sparse_in, low_ref, sparse_out,
+    a_ref, x_ref, a3, xl, xr, wl, res_ref, sparse_ref, in_sems, out_sems,
+):
+    ins = moves(((res_in, res_ref), (sparse_in, sparse_ref)), in_sems)
+    put_inverse(cov_ref, scales_ref, a_ref, x_ref, a3, xl, xr, wl)
+    for copy in ins:
+        copy.wait()
+    outs = moves(((sparse_ref, sparse_out),), out_sems)
     low_ref[...] = low_of(res_ref, xl, xr)
-    copy.wait()
+    outs[0].wait()
 
 
 VM = pl.BlockSpec(memory_space=pltpu.VMEM)
 SM = pl.BlockSpec(memory_space=pltpu.SMEM)
+HBM = pl.BlockSpec(memory_space=pl.ANY)
 
 
 def inverse_scratch():
@@ -293,6 +315,7 @@
         pltpu.VMEM((3 * NCH, NCH), BF16),
         pltpu.VMEM((NCH, 3 * NCH), BF16),
         pltpu.VMEM((3 * NCH, NCH), BF16),
+        pltpu.VMEM((NCH, 3 * NCH), BF16),
     ]
 
 
@@ -307,8 +330,11 @@
             jax.ShapeDtypeStruct((ROWS, 128), F32),
         ),
         in_specs=[VM, VM],
-        out_specs=(VM, VM, VM),
-        scratch_shapes=[pltpu.VMEM((3 * pix, NCH), BF16), pltpu.VMEM((3 * pix, NCH), BF16)] + reduce_scratch(),
+        out_specs=(HBM, HBM, VM),
+        scratch_shapes=[pltpu.VMEM((3 * pix, NCH), BF16)] * 2
+        + [pltpu.VMEM((pix, NCH), F32)] * 2
+        + [pltpu.SemaphoreType.DMA((2,))]
+        + reduce_scratch(),
         compiler_params=pltpu.CompilerParams(collective_id=2, has_side_effects=True),
     )(parts, thr)
 
@@ -323,9 +349,12 @@
             jax.ShapeDtypeStruct((pix, NCH), F32),
             jax.ShapeDtypeStruct((ROWS, 128), F32),
         ),
-        in_specs=[SM, VM, VM, VM, VM],
-        out_specs=(VM, VM, VM),
-        scratch_shapes=inverse_scratch() + reduce_scratch(),
+        in_specs=[SM, VM, HBM, HBM, VM],
+        out_specs=(HBM, HBM, VM),
+        scratch_shapes=inverse_scratch()
+        + [pltpu.VMEM((pix, NCH), F32)] * 4
+        + [pltpu.SemaphoreType.DMA((2,))] * 2
+        + reduce_scratch(),
         compiler_params=pltpu.CompilerParams(collective_id=3, has_side_effects=True),
     )(scales, cov, res, sky, thr)
 
@@ -335,9 +364,11 @@
         last_kernel,
         name="last_stage",
         out_shape=(jax.ShapeDtypeStruct(res.shape, F32), jax.ShapeDtypeStruct(res.shape, F32)),
-        in_specs=[SM, VM, VM, VM],
-        out_specs=(VM, pl.BlockSpec(memory_space=pl.ANY)),
-        scratch_shapes=inverse_scratch() + [pltpu.SemaphoreType.DMA],
+        in_specs=[SM, VM, HBM, HBM],
+        out_specs=(VM, HBM),
+        scratch_shapes=inverse_scratch()
+        + [pltpu.VMEM(res.shape, F32)] * 2
+        + [pltpu.SemaphoreType.DMA((2,)), pltpu.SemaphoreType.DMA((1,))],
     )(scales, cov, res, sparse)
 
 

time: 148 us -> 144 us (0.973)
  Pallas kernels: 147 us -> 143 us
    pallas_call x1, Pallas kernels: 42.5 us -> 40.2 us  [middle_stage(): pl.pallas_call(middle_kernel, name='middle_stage', out_shape=(jax.ShapeDt...]
    pallas_call x1, Pallas kernels: 18.1 us -> 16.5 us  [last_stage(): pl.pallas_call(last_kernel, name='last_stage', out_shape=(jax.ShapeDtypeS...]
where the time goes in v4:
time: 144 us
  Pallas kernels  143 us (99%)
    pallas_call x1, Pallas kernels, front_stage(): pl.pallas_call(front_kernel, name='front_stage', out_shape=jax.ShapeDtype...  57.6 us
    pallas_call x1, Pallas kernels, middle_stage(): pl.pallas_call(middle_kernel, name='middle_stage', out_shape=(jax.ShapeDt...  40.2 us
    pallas_call x1, Pallas kernels, first_stage(): pl.pallas_call(first_kernel, name='first_stage', out_shape=(jax.ShapeDtyp...  28.6 us
    pallas_call x1, Pallas kernels, last_stage(): pl.pallas_call(last_kernel, name='last_stage', out_shape=(jax.ShapeDtypeS...  16.5 us

profile of v4, /device:TPU:1, one launch (start us, length us, event | category | flops | bytes accessed | tf_op | source)
XLA Modules:
  0.0 143.8 jit_solution(9144369486338893852)
XLA Ops:
  0.6 57.6 %front_stage.1.parts_ref = f32[4,512,128]{2,1,0:T(8,128)} custom-call(s32[1024]{0:T(1024)} %ord_ref.1, s32[1,1024]{1,0:T(1,128)} %bitcast.4, bf16[16,64,1024]{2,1,0:T(8,128)(2,1)} %leg_hbm.1, bf16[2,16,1024,128]{3,2,1,0:T(8,128)(2,1)} %co_hbm.1), custom_call_target="tpu_custom_call" | custom-call | tf_op jit(solution)/shard_map/front_stage/pallas_call | solution.py:537
  58.2 28.6 %first_stage.1 = (f32[512,512]{1,0:T(8,128)}, f32[512,512]{1,0:T(8,128)}, f32[1280,128]{1,0:T(8,128)}) custom-call(f32[4,512,128]{2,1,0:T(8,128)} %front_stage.1.parts_ref, f32[1,512]{1,0:T(1,128)} %bitcast.5), custom_call_target="tpu_custom_call" | custom-call | tf_op jit(solution)/shard_map/first_stage/pallas_call | solution.py:324
  86.8 40.2 %middle_stage.1 = (f32[512,512]{1,0:T(8,128)}, f32[512,512]{1,0:T(8,128)}, f32[1280,128]{1,0:T(8,128)}) custom-call(f32[16]{0:T(128)} %constant.2.clone.scales_ref, f32[1280,128]{1,0:T(8,128)} %get-tuple-element.10.cov_ref, f32[512,512]{1,0:T(8,128)} %get-tuple-element.11.res_in, f32[512,512]{1,0:T(8,128)} %get-tuple-element.12.sky_in, f32[1,512]{1,0:T(1,128)} %bitcast.6), custom_call_target="tpu_custom_call" | custom-call | tf_op jit(solution)/shard_map/middle_stage/pallas_call | solution.py:344
  127.1 16.5 %last_stage.1 = (f32[512,512]{1,0:T(8,128)}, f32[512,512]{1,0:T(8,128)}) custom-call(f32[16]{0:T(128)} %constant.2.clone.scales_ref, f32[1280,128]{1,0:T(8,128)} %get-tuple-element.13.cov_ref, f32[512,512]{1,0:T(8,128)} %get-tuple-element.14.res_in, f32[512,512]{1,0:T(8,128)} %get-tuple-element.15.sparse_in), custom_call_target="tpu_custom_call" | custom-call | tf_op jit(solution)/shard_map/last_stage/pallas_call | solution.py:363

commit v5 on v4

--- a/solution.py
+++ b/solution.py
@@ -83,6 +83,9 @@
     return x, y, core, other, partner, plane, deep
 
 
+GREETED = X * Y + Z - 1
+
+
 def greet():
     _, _, _, _, partner, plane, deep = reduce_peers()
     barrier = pltpu.get_barrier_semaphore()
@@ -92,7 +95,6 @@
 
 def reduce_all(p_ref, out_ref, b1, acc1, b2, acc2, b3, acc3, s1, r1, s2, r2, s3, r3, s4, r4, s5, r5):
     x, y, core, other, partner, plane, deep = reduce_peers()
-    pl.semaphore_wait(pltpu.get_barrier_semaphore(), X * Y + Z - 1)
 
     order = sorted(range(X * Y), key=lambda k: -(min(k // Y, X - k // Y) + min(k % Y, Y - k % Y)))
 
@@ -204,8 +206,7 @@
     return copies
 
 
-def first_kernel(parts_ref, thr_ref, sky_out, res_out, cov_ref, left, right, sky_ref, res_ref, sems, part_ref, *reduce_refs):
-    greet()
+def first_body(parts_ref, thr_ref, sky_out, res_out, cov_ref, left, right, sky_ref, res_ref, sems, part_ref, *reduce_refs):
     thr = thr_ref[...]
     sky = jnp.concatenate([parts_ref[i] for i in range(NB)], axis=1)
     sky_ref[...] = sky
@@ -285,6 +286,7 @@
     res2_ref[...] = res
     put_cov(res, part_ref, a3, xr)
     outs = moves(((sparse_ref, sparse_out), (res2_ref, res2_out)), out_sems)
+    pl.semaphore_wait(pltpu.get_barrier_semaphore(), GREETED)
     reduce_all(part_ref, cov2_ref, *reduce_refs)
     for copy in outs:
         copy.wait()
@@ -317,26 +319,6 @@
         pltpu.VMEM((3 * NCH, NCH), BF16),
         pltpu.VMEM((NCH, 3 * NCH), BF16),
     ]
-
-
-def first_stage(parts, thr):
-    pix = parts.shape[1]
-    return pl.pallas_call(
-        first_kernel,
-        name="first_stage",
-        out_shape=(
-            jax.ShapeDtypeStruct((pix, NCH), F32),
-            jax.ShapeDtypeStruct((pix, NCH), F32),
-            jax.ShapeDtypeStruct((ROWS, 128), F32),
-        ),
-        in_specs=[VM, VM],
-        out_specs=(HBM, HBM, VM),
-        scratch_shapes=[pltpu.VMEM((3 * pix, NCH), BF16)] * 2
-        + [pltpu.VMEM((pix, NCH), F32)] * 2
-        + [pltpu.SemaphoreType.DMA((2,))]
-        + reduce_scratch(),
-        compiler_params=pltpu.CompilerParams(collective_id=2, has_side_effects=True),
-    )(parts, thr)
 
 
 def middle_stage(scales, cov, res, sky, thr):
@@ -380,9 +362,9 @@
 
 
 def front_kernel(
-    ord_ref, row_ref, leg_hbm, co_hbm, out_ref,
+    ord_ref, row_ref, leg_hbm, co_hbm, thr_ref, sky_out, res_out, cov_ref, out_ref,
     leg_v, co_v, sp, rb, th, tl, trig_a, trig_b, par, rhs, stage,
-    ls, s1, r1, s2, r2,
+    ls, s1, r1, s2, r2, *first_refs,
 ):
     slots, cycles, degrees = leg_v.shape
     total = WIDE * slots
@@ -417,6 +399,7 @@
             copy.start()
 
     barrier = pltpu.get_barrier_semaphore()
+    greet()
     for o in offsets:
         pl.semaphore_signal(barrier, inc=1, device_id=(at(1, o), y), device_id_type=MESH)
     for d in range(1, Y):
@@ -440,7 +423,7 @@
             for k in range(2):
                 sp[g, pl.ds(k * gs + t, cycles, stride=2 * gs), :] = value[:, k * 128 : (k + 1) * 128]
         if g == 0:
-            pl.semaphore_wait(barrier, len(offsets) + Y - 1)
+            pl.semaphore_wait(barrier, len(offsets) + Y - 1 + GREETED)
         for r, o in enumerate(offsets):
             to = at(1, o)
             sends[g, r] = remote(
@@ -521,26 +504,31 @@
                     outs[q, b].start()
     for copy in outs.values():
         copy.wait_recv()
+    first_body(out_ref, thr_ref, sky_out, res_out, cov_ref, *first_refs)
     for copy in outs.values():
         copy.wait_send()
     for copy in sends.values():
         copy.wait_send()
 
 
-def front_stage(order_table, legendre, coeffs):
+def front_stage(order_table, legendre, coeffs, thr):
     slots, cycles, degrees = legendre.shape
     total = WIDE * slots
     gs = slots // GROUPS
     width = NPIX // Y
     dma = pltpu.SemaphoreType.DMA
-    hbm = pl.BlockSpec(memory_space=pl.ANY)
     return pl.pallas_call(
         front_kernel,
         name="front_stage",
-        out_shape=jax.ShapeDtypeStruct((Y, width, 128), F32),
-        in_specs=[SM, VM, hbm, hbm],
-        out_specs=VM,
+        out_shape=(
+            jax.ShapeDtypeStruct((width, NCH), F32),
+            jax.ShapeDtypeStruct((width, NCH), F32),
+            jax.ShapeDtypeStruct((ROWS, 128), F32),
+        ),
+        in_specs=[SM, VM, HBM, HBM, VM],
+        out_specs=(HBM, HBM, VM),
         scratch_shapes=[
+            pltpu.VMEM((Y, width, 128), F32),
             pltpu.VMEM((slots, cycles, degrees), BF16),
             pltpu.VMEM((slots, degrees, 256), BF16),
             pltpu.VMEM((GROUPS, cycles * 2 * gs, 128), F32),
@@ -557,16 +545,21 @@
             dma((GROUPS, WIDE)),
             dma((Y, SUBS)),
             dma((Y, SUBS)),
-        ],
+            pltpu.VMEM((3 * width, NCH), BF16),
+            pltpu.VMEM((3 * width, NCH), BF16),
+            pltpu.VMEM((width, NCH), F32),
+            pltpu.VMEM((width, NCH), F32),
+            dma((2,)),
+        ]
+        + reduce_scratch(),
         compiler_params=pltpu.CompilerParams(collective_id=1, has_side_effects=True),
-    )(order_table, order_table[None, :], legendre, coeffs)
+    )(order_table, order_table[None, :], legendre, coeffs, thr)
 
 
 def per_device(coeffs, legendre, order_table, thresholds):
-    parts = front_stage(order_table, legendre, coeffs)
     thr = thresholds[None, :]
     scales = jnp.asarray(SCALES + [0.0] * (16 - len(SCALES)), F32)
-    sky, res, cov = first_stage(parts, thr)
+    sky, res, cov = front_stage(order_table, legendre, coeffs, thr)
     sparse, res, cov = middle_stage(scales, cov, res, sky, thr)
     low, sparse = last_stage(scales, cov, res, sparse)
     return low[None], sparse[None]

time: 144 us -> 138 us (0.958)
  Pallas kernels: 143 us -> 137 us
    pallas_call x2 -> x1, Pallas kernels: 86.2 us -> 81.5 us  [front_stage(): pl.pallas_call(front_kernel, name='front_stage', out_shape=(jax.ShapeDtyp...]
where the time goes in v5:
time: 138 us
  Pallas kernels  137 us (99%)
    pallas_call x1, Pallas kernels, front_stage(): pl.pallas_call(front_kernel, name='front_stage', out_shape=(jax.ShapeDtyp...  81.5 us
    pallas_call x1, Pallas kernels, middle_stage(): pl.pallas_call(middle_kernel, name='middle_stage', out_shape=(jax.ShapeDt...  39.1 us
    pallas_call x1, Pallas kernels, last_stage(): pl.pallas_call(last_kernel, name='last_stage', out_shape=(jax.ShapeDtypeS...  16.5 us

profile of v5, /device:TPU:1, one launch (start us, length us, event | category | flops | bytes accessed | tf_op | source)
XLA Modules:
  0.0 138.0 jit_solution(10524754257231129510)
XLA Ops:
  0.6 81.5 %front_stage.1 = (f32[512,512]{1,0:T(8,128)}, f32[512,512]{1,0:T(8,128)}, f32[1280,128]{1,0:T(8,128)}) custom-call(s32[1024]{0:T(1024)} %ord_ref.1, s32[1,1024]{1,0:T(1,128)} %bitcast.4, bf16[16,64,1024]{2,1,0:T(8,128)(2,1)} %leg_hbm.1, bf16[2,16,1024,128]{3,2,1,0:T(8,128)(2,1)} %co_hbm.1, f32[1,512]{1,0:T(1,128)} %bitcast.5), custom_call_target="tpu_custom_call" | custom-call | tf_op jit(solution)/shard_map/front_stage/pallas_call | solution.py:520
  82.2 39.1 %middle_stage.1 = (f32[512,512]{1,0:T(8,128)}, f32[512,512]{1,0:T(8,128)}, f32[1280,128]{1,0:T(8,128)}) custom-call(f32[16]{0:T(128)} %constant.2.clone.scales_ref, f32[1280,128]{1,0:T(8,128)} %get-tuple-element.10.cov_ref, f32[512,512]{1,0:T(8,128)} %get-tuple-element.11.res_in, f32[512,512]{1,0:T(8,128)} %get-tuple-element.12.sky_in, f32[1,512]{1,0:T(1,128)} %bitcast.6), custom_call_target="tpu_custom_call" | custom-call | tf_op jit(solution)/shard_map/middle_stage/pallas_call | solution.py:326
  121.3 16.5 %last_stage.1 = (f32[512,512]{1,0:T(8,128)}, f32[512,512]{1,0:T(8,128)}) custom-call(f32[16]{0:T(128)} %constant.2.clone.scales_ref, f32[1280,128]{1,0:T(8,128)} %get-tuple-element.13.cov_ref, f32[512,512]{1,0:T(8,128)} %get-tuple-element.14.res_in, f32[512,512]{1,0:T(8,128)} %get-tuple-element.15.sparse_in), custom_call_target="tpu_custom_call" | custom-call | tf_op jit(solution)/shard_map/last_stage/pallas_call | solution.py:345
